TPU v7x, 32 devices: a whole 2x2x4 slice. The times are simulated.
32 devices in a mesh: row: 8 (over y, x, core), col: 4 (over z).
Axes of the slice: x: 2, y: 2, z: 4, core: 2. Of those that a mesh axis runs over, the one named last changes fastest.
Arguments:
- inputs_act: bfloat16 [1024, 4096], P('row', 'col'), may hold values from -6 to 6
- out_grad: bfloat16 [1024, 4096], P('row', 'col'), may hold values from -6 to 6
- pre_act: bfloat16 [1024, 16384], P('col', 'row'), may hold values from -8 to 8
- w_first: bfloat16 [4096, 16384], P('col', 'row'), may hold values from -0.046875 to 0.046875
- w_second: bfloat16 [16384, 4096], P('row', 'col'), may hold values from -0.09375 to 0.09375
Outputs:
- grad_input: bfloat16 [1024, 4096], P('row', 'col')
- grad_first: float32 [4096, 16384], P('col', 'row')
- grad_second: float32 [16384, 4096], P('row', 'col')
All inputs are finite; a program needn't handle non-finite values.
Results may differ from a plain program's by a relative error of at most 0.019.
Values may be sent and summed in bfloat16 or wider, within the bound.
A program may use at most 128 MiB of HBM per device.

v0:
```python
import math
import jax
import jax.numpy as jnp
from jax import lax
from jax.sharding import PartitionSpec as P

gelu_coef = 0.044715


def gelu_pair(pre_float):
    inner_c = math.sqrt(2.0 / math.pi)
    inner = inner_c * (pre_float + gelu_coef * pre_float * pre_float * pre_float)
    tanh_val = jnp.tanh(inner)
    act = 0.5 * pre_float * (1.0 + tanh_val)
    slope = 0.5 * (1.0 + tanh_val) + 0.5 * pre_float * (1.0 - tanh_val * tanh_val) * inner_c * (
        1.0 + 3.0 * gelu_coef * pre_float * pre_float
    )
    return (act, slope)


def contract_last(left, right):
    return lax.dot_general(
        left, right, (((1,), (1,)), ((), ())), preferred_element_type=jnp.float32
    )


def contract_first(left, right):
    return lax.dot_general(
        left, right, (((0,), (0,)), ((), ())), preferred_element_type=jnp.float32
    )


def on_device(inputs_act, out_grad, pre_act, w_first, w_second):
    total_tokens = pre_act.shape[0] * lax.axis_size("col")
    factor = 1.0 / math.sqrt(total_tokens)
    x_whole, dy_whole = (
        lax.all_gather(inputs_act, "row", axis=0, tiled=True),
        lax.all_gather(out_grad, "row", axis=0, tiled=True),
    )
    hidden_whole = lax.psum(contract_last(dy_whole, w_second).astype(jnp.bfloat16), "col").astype(
        jnp.float32
    )
    pre_whole = lax.all_gather(pre_act, "col", axis=0, tiled=True)
    act_float, slope = gelu_pair(pre_whole.astype(jnp.float32))
    act_whole = act_float.astype(jnp.bfloat16)
    grad_whole = (hidden_whole * slope).astype(jnp.bfloat16)
    grad_input = lax.psum_scatter(
        contract_last(grad_whole, w_first).astype(jnp.bfloat16),
        "row",
        scatter_dimension=0,
        tiled=True,
    )
    grad_first = contract_first(x_whole, grad_whole) * factor
    grad_second = contract_first(act_whole, dy_whole) * factor
    return (grad_input, grad_first, grad_second)


def solution(mesh):
    in_specs = (P("row", "col"), P("row", "col"), P("col", "row"), P("col", "row"), P("row", "col"))
    out_specs = (P("row", "col"), P("col", "row"), P("row", "col"))
    return jax.shard_map(
        on_device, mesh=mesh, in_specs=in_specs, out_specs=out_specs, check_vma=False
    )
```

profile of v0, /device:TPU:0, one launch (start us, length us, event | category | flops | bytes accessed | tf_op | source)
XLA Modules:
  0.0 360.1 jit_solution(10771306066762961557)
XLA Ops:
  7.2 0.0 all-gather.4.cloned.1.call-start
  7.2 0.7 all-gather.4.cloned.1.call-update
  7.9 0.0 all-gather.6.cloned.1.call-start
  7.9 0.7 all-gather.6.cloned.1.call-update
  8.6 0.0 all-reduce.2.cloned.1.call-start
  8.7 31.8 %all-gather.4.cloned.1.call-done = bf16[1024,1024]{1,0:T(8,128)(2,1)} async-done(((bf16[128,1024]{1,0:T(8,128)(2,1)}), bf16[1024,1024]{1,0:T(8,128)(2,1)}) %all-gather.4.cloned.1.call-update) | async-done | bytes 2097168 | tf_op jit(solution)/shard_map/all_gather | solution.py:38
  40.5 9.4 %convolution_convert_fusion = bf16[1024,2048]{1,0:T(8,128)(2,1)} fusion(bf16[1024,1024]{1,0:T(8,128)(2,1)} %all-gather.4.cloned.1.call-done, bf16[2048,1024]{1,0:T(8,128)(2,1)} %param.9), kind=kOutput, calls=%fused_computation.24 | convolution fusion | flops 4297064448 | bytes 10485760 | tf_op jit(solution)/shard_map/dot_general | solution.py:22
  49.9 0.0 all-reduce.2.cloned.1.call-update
  49.9 0.0 all-gather.8.cloned.1.call-start
  50.0 0.5 all-gather.8.cloned.1.call-update
  50.5 0.0 reduce-scatter.2.cloned.1.call-start
  50.5 72.3 %all-gather.6.cloned.1.call-done = bf16[1024,2048]{1,0:T(8,128)(2,1)} async-done(((bf16[256,2048]{1,0:T(8,128)(2,1)}), bf16[1024,2048]{1,0:T(8,128)(2,1)}) %all-gather.6.cloned.1.call-update) | async-done | bytes 4194320 | tf_op jit(solution)/shard_map/all_gather | solution.py:43
  122.9 156.5 %all-reduce.2.cloned.1.call-done = bf16[1024,2048]{1,0:T(8,128)(2,1)} async-done(((bf16[1024,2048]{1,0:T(8,128)(2,1)}), bf16[1024,2048]{1,0:T(8,128)(2,1)}) %all-reduce.2.cloned.1.call-update) | async-done | bytes 4194320 | tf_op jit(solution)/shard_map/psum | solution.py:40
  279.4 0.0 copy-start.1
  279.4 8.2 %fusion.6 = bf16[1024,2048]{1,0:T(8,128)(2,1)S(1)} fusion(bf16[1024,2048]{1,0:T(8,128)(2,1)} %all-gather.6.cloned.1.call-done, bf16[1024,2048]{1,0:T(8,128)(2,1)} %all-reduce.2.cloned.1.call-done), kind=kLoop, calls=%fused_computation.13 | loop fusion | flops 44040192 | bytes 12582912 | tf_op jit(solution)/shard_map/convert_element_type | solution.py:46
  287.6 0.0 copy-start
  287.6 2.0 copy-done
  289.6 0.0 copy-done.1
  289.6 0.0 copy-start.2
  289.6 5.7 %convolution_convert_fusion.1 = bf16[1024,1024]{1,0:T(8,128)(2,1)} fusion(bf16[1024,2048]{1,0:T(8,128)(2,1)S(1)} %fusion.6, bf16[1024,2048]{1,0:T(8,128)(2,1)S(1)} %copy-done.1), kind=kOutput, calls=%fused_computation.25 | convolution fusion | flops 4296015872 | bytes 10485760 | tf_op jit(solution)/shard_map/dot_general | solution.py:22
  295.4 0.0 reduce-scatter.2.cloned.1.call-update
  295.4 0.0 copy-done.2
  295.4 12.1 %convolution_multiply_fusion = f32[2048,1024]{1,0:T(8,128)} fusion(bf16[1024,1024]{1,0:T(8,128)(2,1)S(1)} %copy-done.2, bf16[1024,2048]{1,0:T(8,128)(2,1)} %all-gather.6.cloned.1.call-done), kind=kOutput, calls=%fused_computation.19 | convolution fusion | flops 4318035968 | bytes 14680064 | tf_op jit(solution)/shard_map/dot_general | solution.py:28
  307.5 0.7 all-gather.8.cloned.1.call-done
  308.2 10.6 %multiply_bitcast_fusion = f32[1024,2048]{0,1:T(8,128)} fusion(bf16[1024,2048]{1,0:T(8,128)(2,1)} %copy-done, bf16[1024,1024]{1,0:T(8,128)(2,1)} %all-gather.8.cloned.1.call-done), kind=kOutput, calls=%fused_computation.18 | convolution fusion | flops 4297064448 | bytes 14680064 | tf_op jit(solution)/shard_map/dot_general | solution.py:28
  318.9 9.3 %copy.8 = f32[1024,2048]{1,0:T(8,128)} copy(f32[1024,2048]{0,1:T(8,128)} %multiply_bitcast_fusion) | data formatting | bytes 16777216
  328.2 25.3 %reduce-scatter.2.cloned.1.call-done = bf16[128,1024]{1,0:T(8,128)(2,1)} async-done(((bf16[1024,1024]{1,0:T(8,128)(2,1)}), bf16[128,1024]{1,0:T(8,128)(2,1)}) %reduce-scatter.2.cloned.1.call-update) | async-done | bytes 262160 | tf_op jit(solution)/shard_map/reduce_scatter | solution.py:47
Async XLA Ops:
  7.2 33.4 %all-gather.4.cloned.1.call-start = ((), (), s32[]{:S(2)}) async-start(), calls=%async_computation.1 | async-start | bytes 2359296 | tf_op jit(solution)/shard_map/all_gather | solution.py:38
  7.9 115.0 %all-gather.6.cloned.1.call-start = ((), (), s32[]{:S(2)}) async-start(), calls=%async_computation.3 | async-start | bytes 5242880 | tf_op jit(solution)/shard_map/all_gather | solution.py:43
  8.6 270.7 %all-reduce.2.cloned.1.call-start = ((), (), s32[]{:S(2)}) async-start(), calls=%async_computation.2 | async-start | bytes 8388608 | tf_op jit(solution)/shard_map/psum | solution.py:40
  49.9 258.3 %all-gather.8.cloned.1.call-start = ((), (), s32[]{:S(2)}) async-start(), calls=%async_computation.5 | async-start | bytes 2359296 | tf_op jit(solution)/shard_map/all_gather | solution.py:37
  50.5 303.0 %reduce-scatter.2.cloned.1.call-start = ((), (), s32[]{:S(2)}) async-start(), calls=%async_computation.4 | async-start | bytes 2359296 | tf_op jit(solution)/shard_map/reduce_scatter | solution.py:47
  279.4 10.3 %copy-start.1 = (bf16[1024,2048]{1,0:T(8,128)(2,1)S(1)}, bf16[1024,2048]{1,0:T(8,128)(2,1)}, u32[]{:S(2)}) copy-start(bf16[1024,2048]{1,0:T(8,128)(2,1)} %param.8) | copy-start | bytes 12582916
  287.6 2.0 copy-start
  289.6 5.8 %copy-start.2 = (bf16[1024,1024]{1,0:T(8,128)(2,1)S(1)}, bf16[1024,1024]{1,0:T(8,128)(2,1)}, u32[]{:S(2)}) copy-start(bf16[1024,1024]{1,0:T(8,128)(2,1)} %all-gather.4.cloned.1.call-done) | copy-start | bytes 6291460
Sparse Core Ops, SparseCore 0:
  9.9 30.5 all-gather.3
  42.1 80.7 all-gather.5
  125.8 153.4 all-reduce.1
  281.3 26.8 all-gather.7
  312.3 41.2 reduce-scatter.1
where the time goes:
time: 360 us
  waiting for transfers between devices  289 us (80%)
  matrix products  37.8 us (10%)
  between operations  13.8 us (4%)
  local copies, waits for them, and re-layouts  11.3 us (3%)
  other arithmetic  8.23 us (2%)
    psum x1, waiting for transfers between devices, on_device(): lax.psum(contract_last(dy_whole, w_second).astype(jnp.bfloat16), 'col')  156 us
    all_gather x1, waiting for transfers between devices, on_device(): pre_whole = lax.all_gather(pre_act, 'col', axis=0, tiled=True)  72.3 us
    all_gather x1, waiting for transfers between devices, on_device(): lax.all_gather(out_grad, 'row', axis=0, tiled=True)  31.8 us
    reduce_scatter x1, waiting for transfers between devices, on_device(): lax.psum_scatter(contract_last(grad_whole, w_first).astype(jnp.bfloat16),...  25.3 us
    dot_general x2, matrix products, contract_first(): lax.dot_general(left, right, (((0,), (0,)), ((), ())), preferred_element_...  22.7 us
    dot_general x2, matrix products, contract_last(): lax.dot_general(left, right, (((1,), (1,)), ((), ())), preferred_element_...  15.1 us
    unnamed x7, local copies, waits for them, and re-layouts  11.3 us
    convert_element_type x1, other arithmetic, on_device(): grad_whole = (hidden_whole * slope).astype(jnp.bfloat16)  8.23 us
  transfers between devices with their start and end apart: 5, of which 5 were waited for; matrix products, arithmetic and copies ran while one was open for 15% of the time, Pallas kernels for 0%

commit v1 on v0

--- a/solution.py
+++ b/solution.py
@@ -40,7 +40,12 @@
     hidden_whole = lax.psum(contract_last(dy_whole, w_second).astype(jnp.bfloat16), "col").astype(
         jnp.float32
     )
-    pre_whole = lax.all_gather(pre_act, "col", axis=0, tiled=True)
+    ring = [pre_act]
+    for hop in range(3):
+        ring.append(lax.ppermute(ring[-1], "col", [(dev, (dev + 1) % 4) for dev in range(4)]))
+    pre_whole = jnp.roll(
+        jnp.concatenate(ring[::-1], axis=0), (lax.axis_index("col") + 1) * ring[0].shape[0], axis=0
+    )
     act_float, slope = gelu_pair(pre_whole.astype(jnp.float32))
     act_whole = act_float.astype(jnp.bfloat16)
     grad_whole = (hidden_whole * slope).astype(jnp.bfloat16)

time: 360 us -> 340 us (0.944)
  waiting for transfers between devices: 289 us -> 233 us
  starting transfers between devices: 0.19 us -> 24.3 us
  local copies, waits for them, and re-layouts: 11.3 us -> 22.2 us
    ppermute x0 -> x3, waiting for transfers between devices: none -> 133 us  [on_device(): lax.ppermute(ring[-1], 'col', [(dev, (dev + 1) % 4) for dev in range(4)])]
    psum x1, waiting for transfers between devices: 156 us -> 41.3 us  [on_device(): lax.psum(contract_last(dy_whole, w_second).astype(jnp.bfloat16), 'col')]
    all_gather x1 -> x0, waiting for transfers between devices: 72.3 us -> none  [on_device(): pre_whole = lax.all_gather(pre_act, 'col', axis=0, tiled=True)]
    ppermute x0 -> x3, starting transfers between devices: none -> 24.1 us  [on_device(): lax.ppermute(ring[-1], 'col', [(dev, (dev + 1) % 4) for dev in range(4)])]
    unnamed x7 -> x16, local copies, waits for them, and re-layouts: 11.3 us -> 21.2 us
  transfers between devices with their start and end apart: 5 -> 7, of which waited for: 5 -> 6; matrix products, arithmetic and copies ran while one was open for 15% -> 17% of each run, Pallas kernels for 0% -> 0%
where the time goes in v1:
time: 340 us
  waiting for transfers between devices  233 us (69%)
  matrix products  37.8 us (11%)
  starting transfers between devices  24.3 us (7%)
  local copies, waits for them, and re-layouts  22.2 us (7%)
  between operations  13.8 us (4%)
  other arithmetic  8.23 us (2%)
    ppermute x3, waiting for transfers between devices, on_device(): lax.ppermute(ring[-1], 'col', [(dev, (dev + 1) % 4) for dev in range(4)])  133 us
    psum x1, waiting for transfers between devices, on_device(): lax.psum(contract_last(dy_whole, w_second).astype(jnp.bfloat16), 'col')  41.3 us
    all_gather x1, waiting for transfers between devices, on_device(): lax.all_gather(out_grad, 'row', axis=0, tiled=True)  32.6 us
    reduce_scatter x1, waiting for transfers between devices, on_device(): lax.psum_scatter(contract_last(grad_whole, w_first).astype(jnp.bfloat16),...  25.3 us
    ppermute x3, starting transfers between devices, on_device(): lax.ppermute(ring[-1], 'col', [(dev, (dev + 1) % 4) for dev in range(4)])  24.1 us
    dot_general x2, matrix products, contract_first(): lax.dot_general(left, right, (((0,), (0,)), ((), ())), preferred_element_...  22.7 us
    unnamed x16, local copies, waits for them, and re-layouts  21.2 us
    dot_general x2, matrix products, contract_last(): lax.dot_general(left, right, (((1,), (1,)), ((), ())), preferred_element_...  15.1 us
  transfers between devices with their start and end apart: 7, of which 6 were waited for; matrix products, arithmetic and copies ran while one was open for 17% of the time, Pallas kernels for 0%

profile of v1, /device:TPU:0, one launch (start us, length us, event | category | flops | bytes accessed | tf_op | source)
XLA Modules:
  0.0 339.8 jit_solution(818132824753392517)
XLA Ops:
  7.2 0.0 all-gather.3.cloned.1.call-start
  7.2 0.7 all-gather.3.cloned.1.call-update
  7.9 0.0 copy-start.1
  7.9 0.0 all-reduce.2.cloned.1.call-start
  8.0 32.6 %all-gather.3.cloned.1.call-done = bf16[1024,1024]{1,0:T(8,128)(2,1)} async-done(((bf16[128,1024]{1,0:T(8,128)(2,1)}), bf16[1024,1024]{1,0:T(8,128)(2,1)}) %all-gather.3.cloned.1.call-update) | async-done | bytes 2097168 | tf_op jit(solution)/shard_map/all_gather | solution.py:38
  40.5 9.4 %convolution_convert_fusion = bf16[1024,2048]{1,0:T(8,128)(2,1)} fusion(bf16[1024,1024]{1,0:T(8,128)(2,1)} %all-gather.3.cloned.1.call-done, bf16[2048,1024]{1,0:T(8,128)(2,1)} %param.9), kind=kOutput, calls=%fused_computation.24 | convolution fusion | flops 4297064448 | bytes 10485760 | tf_op jit(solution)/shard_map/dot_general | solution.py:22
  49.9 0.0 all-reduce.2.cloned.1.call-update
  49.9 0.0 all-gather.5.cloned.1.call-start
  50.0 0.0 copy-done.1
  50.0 1.5 collective-permute-start
  51.5 44.1 %collective-permute-done = bf16[256,2048]{1,0:T(8,128)(2,1)S(1)} collective-permute-done((bf16[256,2048]{1,0:T(8,128)(2,1)S(1)}, bf16[256,2048]{1,0:T(8,128)(2,1)S(1)}, u32[]{:S(2)}, u32[]{:S(2)}) %collective-permute-start) | collective-permute-done | bytes 1048608 | tf_op jit(solution)/shard_map/ppermute | solution.py:45
  95.6 19.3 %collective-permute-start.1 = (bf16[256,2048]{1,0:T(8,128)(2,1)S(1)}, bf16[256,2048]{1,0:T(8,128)(2,1)S(1)}, u32[]{:S(2)}, u32[]{:S(2)}) collective-permute-start(bf16[256,2048]{1,0:T(8,128)(2,1)S(1)} %collective-permute-done), channel_id=1, source_target_pairs={{0,1},{1,2},{2,3},{3,0},{4,5},{5,6},{6,7},{7,4},{8,9},{9,10},{10,1... | collective-permute-start | bytes 3145736 | tf_op jit(solution)/shard_map/ppermute | solution.py:45
  114.9 47.5 %collective-permute-done.1 = bf16[256,2048]{1,0:T(8,128)(2,1)S(1)} collective-permute-done((bf16[256,2048]{1,0:T(8,128)(2,1)S(1)}, bf16[256,2048]{1,0:T(8,128)(2,1)S(1)}, u32[]{:S(2)}, u32[]{:S(2)}) %collective-permute-start.1) | collective-permute-done | bytes 1048608 | tf_op jit(solution)/shard_map/ppermute | solution.py:45
  162.4 3.3 collective-permute-start.2
  165.7 0.0 all-gather.5.cloned.1.call-update
  165.7 0.0 reduce-scatter.2.cloned.1.call-start
  165.8 41.8 %collective-permute-done.2 = bf16[256,2048]{1,0:T(8,128)(2,1)} collective-permute-done((bf16[256,2048]{1,0:T(8,128)(2,1)S(1)}, bf16[256,2048]{1,0:T(8,128)(2,1)}, u32[]{:S(2)}, u32[]{:S(2)}) %collective-permute-start.2) | collective-permute-done | bytes 1048608 | tf_op jit(solution)/shard_map/ppermute | solution.py:45
  207.7 2.3 constant_dynamic-update-slice_fusion.7
  210.0 1.0 constant_dynamic-update-slice_fusion.6
  211.0 1.0 constant_dynamic-update-slice_fusion.5
  212.0 1.1 constant_dynamic-update-slice_fusion.4
  213.1 2.3 constant_dynamic-update-slice_fusion.3
  215.4 1.0 constant_dynamic-update-slice_fusion.2
  216.5 1.0 constant_dynamic-update-slice_fusion.1
  217.5 1.1 constant_dynamic-update-slice_fusion
  218.6 41.3 %all-reduce.2.cloned.1.call-done = bf16[1024,2048]{1,0:T(8,128)(2,1)} async-done(((bf16[1024,2048]{1,0:T(8,128)(2,1)}), bf16[1024,2048]{1,0:T(8,128)(2,1)}) %all-reduce.2.cloned.1.call-update) | async-done | bytes 4194320 | tf_op jit(solution)/shard_map/psum | solution.py:40
  259.9 0.0 copy-start.2
  259.9 8.2 %fusion.6 = bf16[1024,2048]{1,0:T(8,128)(2,1)S(1)} fusion(bf16[1024,2048]{1,0:T(8,128)(2,1)} %all-reduce.2.cloned.1.call-done, bf16[2048,2048]{1,0:T(8,128)(2,1)} %constant_dynamic-update-slice_fusion, s32[]{:T(128)S(6)} %select_n.14), kind=kLoop, calls=%fused_computation.13 | loop fusion | flops 44040192 | bytes 12582916 | tf_op jit(solution)/shard_map/convert_element_type | solution.py:51
  268.2 0.0 copy-start
  268.2 2.0 copy-done
  270.1 0.0 copy-done.2
  270.1 0.0 copy-start.3
  270.1 5.8 %convolution_convert_fusion.1 = bf16[1024,1024]{1,0:T(8,128)(2,1)} fusion(bf16[1024,2048]{1,0:T(8,128)(2,1)S(1)} %fusion.6, bf16[1024,2048]{1,0:T(8,128)(2,1)S(1)} %copy-done.2), kind=kOutput, calls=%fused_computation.26 | convolution fusion | flops 4296015872 | bytes 10485760 | tf_op jit(solution)/shard_map/dot_general | solution.py:22
  275.9 0.0 reduce-scatter.2.cloned.1.call-update
  275.9 0.0 copy-done.3
  275.9 12.1 %convolution_multiply_fusion = f32[2048,1024]{1,0:T(8,128)} fusion(bf16[1024,1024]{1,0:T(8,128)(2,1)S(1)} %copy-done.3, bf16[2048,2048]{1,0:T(8,128)(2,1)} %constant_dynamic-update-slice_fusion, s32[]{:T(128)S(6)} %select_n.14), kind=kOutput, calls=%fused_computation.19 | convolution fusion | flops 4318035968 | bytes 14680068 | tf_op jit(solution)/shard_map/dot_general | solution.py:28
  288.0 0.0 all-gather.5.cloned.1.call-done
  288.0 10.7 %multiply_bitcast_fusion = f32[1024,2048]{0,1:T(8,128)} fusion(bf16[1024,2048]{1,0:T(8,128)(2,1)} %copy-done, bf16[1024,1024]{1,0:T(8,128)(2,1)} %all-gather.5.cloned.1.call-done), kind=kOutput, calls=%fused_computation.18 | convolution fusion | flops 4297064448 | bytes 14680064 | tf_op jit(solution)/shard_map/dot_general | solution.py:28
  298.7 9.3 %copy.8 = f32[1024,2048]{1,0:T(8,128)} copy(f32[1024,2048]{0,1:T(8,128)} %multiply_bitcast_fusion) | data formatting | bytes 16777216
  308.0 25.3 %reduce-scatter.2.cloned.1.call-done = bf16[128,1024]{1,0:T(8,128)(2,1)} async-done(((bf16[1024,1024]{1,0:T(8,128)(2,1)}), bf16[128,1024]{1,0:T(8,128)(2,1)}) %reduce-scatter.2.cloned.1.call-update) | async-done | bytes 262160 | tf_op jit(solution)/shard_map/reduce_scatter | solution.py:52
Async XLA Ops:
  7.2 33.4 %all-gather.3.cloned.1.call-start = ((), (), s32[]{:S(2)}) async-start(), calls=%async_computation.1 | async-start | bytes 2359296 | tf_op jit(solution)/shard_map/all_gather | solution.py:38
  7.9 42.1 %copy-start.1 = (bf16[256,2048]{1,0:T(8,128)(2,1)S(1)}, bf16[256,2048]{1,0:T(8,128)(2,1)}, u32[]{:S(2)}) copy-start(bf16[256,2048]{1,0:T(8,128)(2,1)} %param.7) | copy-start | bytes 3145732
  7.9 252.0 %all-reduce.2.cloned.1.call-start = ((), (), s32[]{:S(2)}) async-start(), calls=%async_computation.2 | async-start | bytes 8388608 | tf_op jit(solution)/shard_map/psum | solution.py:40
  49.9 238.1 %all-gather.5.cloned.1.call-start = ((), (), s32[]{:S(2)}) async-start(), calls=%async_computation.4 | async-start | bytes 2359296 | tf_op jit(solution)/shard_map/all_gather | solution.py:37
  50.0 45.6 %collective-permute-start = (bf16[256,2048]{1,0:T(8,128)(2,1)S(1)}, bf16[256,2048]{1,0:T(8,128)(2,1)S(1)}, u32[]{:S(2)}, u32[]{:S(2)}) collective-permute-start(bf16[256,2048]{1,0:T(8,128)(2,1)S(1)} %copy-done.1), channel_id=1, source_target_pairs={{0,1},{1,2},{2,3},{3,0},{4,5},{5,6},{6,7},{7,4},{8,9},{9,10},{10,1... | collective-permute-start | bytes 3145736 | tf_op jit(solution)/shard_map/ppermute | solution.py:45
  95.6 66.8 %collective-permute-start.1 = (bf16[256,2048]{1,0:T(8,128)(2,1)S(1)}, bf16[256,2048]{1,0:T(8,128)(2,1)S(1)}, u32[]{:S(2)}, u32[]{:S(2)}) collective-permute-start(bf16[256,2048]{1,0:T(8,128)(2,1)S(1)} %collective-permute-done), channel_id=1, source_target_pairs={{0,1},{1,2},{2,3},{3,0},{4,5},{5,6},{6,7},{7,4},{8,9},{9,10},{10,1... | collective-permute-start | bytes 3145736 | tf_op jit(solution)/shard_map/ppermute | solution.py:45
  162.4 45.2 %collective-permute-start.2 = (bf16[256,2048]{1,0:T(8,128)(2,1)S(1)}, bf16[256,2048]{1,0:T(8,128)(2,1)}, u32[]{:S(2)}, u32[]{:S(2)}) collective-permute-start(bf16[256,2048]{1,0:T(8,128)(2,1)S(1)} %collective-permute-done.1), channel_id=1, source_target_pairs={{0,1},{1,2},{2,3},{3,0},{4,5},{5,6},{6,7},{7,4},{8,9},{9,10},{10,1... | collective-permute-start | bytes 3145736 | tf_op jit(solution)/shard_map/ppermute | solution.py:45
  165.7 167.5 %reduce-scatter.2.cloned.1.call-start = ((), (), s32[]{:S(2)}) async-start(), calls=%async_computation.3 | async-start | bytes 2359296 | tf_op jit(solution)/shard_map/reduce_scatter | solution.py:52
  259.9 10.2 %copy-start.2 = (bf16[1024,2048]{1,0:T(8,128)(2,1)S(1)}, bf16[1024,2048]{1,0:T(8,128)(2,1)}, u32[]{:S(2)}) copy-start(bf16[1024,2048]{1,0:T(8,128)(2,1)} %param.8) | copy-start | bytes 12582916
  268.2 2.0 copy-start
  270.1 5.8 %copy-start.3 = (bf16[1024,1024]{1,0:T(8,128)(2,1)S(1)}, bf16[1024,1024]{1,0:T(8,128)(2,1)}, u32[]{:S(2)}) copy-start(bf16[1024,1024]{1,0:T(8,128)(2,1)} %all-gather.3.cloned.1.call-done) | copy-start | bytes 6291460
Sparse Core Ops, SparseCore 0:
  9.9 30.5 all-gather.2
  50.0 209.8 all-reduce.1
  262.0 25.9 all-gather.4
  292.0 41.2 reduce-scatter.1
